TPU v7x, 32 devices: a whole 2x2x4 slice. The times are simulated.
32 devices in a mesh: dp: 4 (over z), ctx: 2 (over core), tp: 4 (over y, x).
Axes of the slice: x: 2, y: 2, z: 4, core: 2. Of those that a mesh axis runs over, the one named last changes fastest.
Arguments:
- block_in: bfloat16 [8192, 2048], P(('dp', 'ctx')), may hold values from -6 to 6
- query_proj: bfloat16 [2048, 2048], P('dp', 'tp'), may hold values from -0.125 to 0.125
- forget_proj: bfloat16 [2048, 2048], P('dp', 'tp'), may hold values from -0.0625 to 0.0625
- value_proj: bfloat16 [2048, 2048], P('dp', 'tp'), may hold values from -0.125 to 0.125
- outgate_proj: bfloat16 [2048, 2048], P('dp', 'tp'), may hold values from -0.125 to 0.125
- out_proj: bfloat16 [2048, 2048], P('tp', 'dp'), may hold values from -0.125 to 0.125
- ffn_gate: bfloat16 [2048, 5632], P('dp', 'tp'), may hold values from -0.125 to 0.125
- ffn_up: bfloat16 [2048, 5632], P('dp', 'tp'), may hold values from -0.125 to 0.125
- ffn_down: bfloat16 [5632, 2048], P('tp', 'dp'), may hold values from -0.078125 to 0.078125
- first_gain: float32 [2048], replicated, may hold values from 0.5 to 1.5
- second_gain: float32 [2048], replicated, may hold values from 0.5 to 1.5
- group_gain: float32 [2048], P('tp'), may hold values from 0.5 to 1.5
- forget_bias: float32 [2048], P('tp'), may hold values from 3 to 12
- bound_table: float32 [24, 2048], P(None, 'tp'), may hold values from -4 to 4
- layer_index: int32 [1], replicated, may hold values from 1 to 23
- second_start: int32 [4], P('dp'), may hold values from 1 to 2048, as said below
- cotangent: bfloat16 [8192, 2048], P(('dp', 'ctx')), may hold values from -6 to 6
Outputs:
- block_out: bfloat16 [8192, 2048], P(('dp', 'ctx'))
- input_grad: float32 [8192, 2048], P(('dp', 'ctx'))
- query_grad: float32 [2048, 2048], P('dp', 'tp')
- forget_grad: float32 [2048, 2048], P('dp', 'tp')
- value_grad: float32 [2048, 2048], P('dp', 'tp')
- outgate_grad: float32 [2048, 2048], P('dp', 'tp')
- out_proj_grad: float32 [2048, 2048], P('tp', 'dp')
- ffn_gate_grad: float32 [2048, 5632], P('dp', 'tp')
- ffn_up_grad: float32 [2048, 5632], P('dp', 'tp')
- ffn_down_grad: float32 [5632, 2048], P('tp', 'dp')
- first_gain_grad: float32 [2048], replicated
- second_gain_grad: float32 [2048], replicated
- group_gain_grad: float32 [2048], P('tp')
- forget_bias_grad: float32 [2048], P('tp')
- bound_table_grad: float32 [24, 2048], P(None, 'tp')
Inputs may be any that keep to these rules, and one draw needn't show every extreme that they name: second_start[p] is 2048 where pack p is one whole sequence, and otherwise the position inside the pack where its second sequence begins; pack 0 is always one whole sequence and pack 1 always holds two. layer_index names a row of bound_table other than the first.
All inputs are finite; a program needn't handle non-finite values.
Results may differ from a plain program's by a relative error of at most 0.018.
Values may be sent and summed in bfloat16 or wider, within the bound.
No kernel may reach another device: no remote copies, remote signals or barrier semaphores. Data moves between devices by JAX's collectives and lax.ppermute only.
A program may use at most 384 MiB of HBM per device.

v0:
```python
import jax
import jax.numpy as jnp
from jax import lax
from jax.sharding import PartitionSpec as P

HEAD = 128
BLOCK = 32
HIGH = lax.Precision.HIGHEST
EPS_NORM = 1e-06
EPS_GROUP = 1e-05


def carried_in(value, axis, join, neutral):
    count, mine = (lax.axis_size(axis), lax.axis_index(axis))
    pieces = jax.tree.map(lambda part: lax.all_gather(part, axis), value)
    total = jax.tree.map(
        lambda part, zero: jnp.full_like(part, 0) + jnp.asarray(zero, part.dtype), value, neutral
    )

    def hop(position, total):
        longer = join(total, jax.tree.map(lambda part: part[position], pieces))
        return jax.tree.map(lambda new, old: jnp.where(position < mine, new, old), longer, total)

    return lax.fori_loop(0, count - 1, hop, total)


def carried_in_2(array, axis, combine, identity):
    peers, index = (lax.axis_size(axis), lax.axis_index(axis))
    everything = jax.tree.map(
        lambda part, kind: lax.all_gather(part.astype(kind), axis),
        array,
        jax.tree.map(lambda a: jnp.bfloat16 if a.dtype == jnp.float32 else a.dtype, array),
    )
    start = jax.tree.map(
        lambda part, zero: jnp.broadcast_to(jnp.asarray(zero, part.dtype), part.shape),
        array,
        identity,
    )

    def hop(k, before):
        at = peers - 1 - k
        reached = at > index
        new = combine(
            before, jax.tree.map(lambda part, own: part[at].astype(own.dtype), everything, array)
        )
        return jax.tree.map(lambda a, b: jnp.where(reached, a, b), new, before)

    return lax.fori_loop(0, peers, hop, start)


def rms_norm(rows_in, gain_vec):
    return (
        rows_in
        * lax.rsqrt(jnp.mean(rows_in * rows_in, axis=-1, keepdims=True) + EPS_NORM)
        * gain_vec
    )


def head_norm(mixed, pre_gate, gain_vec, head_count):
    row_count = mixed.shape[0]
    grouped = mixed.reshape(row_count, head_count, -1)
    scaled = grouped * lax.rsqrt(jnp.mean(grouped * grouped, axis=-1, keepdims=True) + EPS_GROUP)
    return scaled.reshape(row_count, -1) * gain_vec * jax.nn.silu(pre_gate)


def lower_bound(bound_rows, which_layer):
    weights = jax.nn.softmax(bound_rows, axis=0)
    rising = jnp.cumsum(weights, axis=0) - weights[0:1]
    picked = (
        lax.broadcasted_iota(jnp.int32, (bound_rows.shape[0], 1), 0) == which_layer[0]
    ).astype(bound_rows.dtype)
    return jnp.sum(rising * picked, axis=0)


def gate_values(pre_query, pre_forget, bias_vec, bound_vec):
    shifted = pre_forget + bias_vec
    forget = bound_vec + (1.0 - bound_vec) * jax.nn.sigmoid(shifted)
    return (jax.nn.silu(pre_query), (1.0 - bound_vec) * jax.nn.sigmoid(-shifted), jnp.log(forget))


def chain_link(earlier, later):
    return (earlier[0] * later[0], later[0][..., None] * earlier[1] + later[1])


def contract_last(left_side, right_side):
    return lax.dot_general(
        left_side, right_side, (((1,), (1,)), ((), ())), preferred_element_type=jnp.float32
    )


def contract_first(left_side, right_side):
    return lax.dot_general(
        left_side, right_side, (((0,), (0,)), ((), ())), preferred_element_type=jnp.float32
    )


def block_parts(queries, key_rows, values, log_forget, doc_ids, prev_doc, block_len):
    length, head_count, feature = queries.shape
    block_count = length // block_len
    blocked = (block_count, block_len, head_count, feature)
    queries = queries.reshape(blocked)
    key_rows = key_rows.reshape(blocked)
    values = values.reshape(blocked)
    decays = jnp.cumsum(log_forget.reshape(blocked), axis=1)
    doc_ids = doc_ids.reshape(block_count, block_len)
    before = jnp.concatenate([jnp.reshape(prev_doc, (1,)), doc_ids[:-1, block_len - 1]])
    middle = decays[:, block_len // 2 : block_len // 2 + 1]
    final_decay = decays[:, block_len - 1 :]
    scores = jnp.einsum(
        "nthc,nshc->nhts",
        queries * jnp.exp(decays - middle),
        key_rows * jnp.exp(middle - decays),
        precision=HIGH,
    )
    causal = lax.broadcasted_iota(jnp.int32, (block_len, block_len), 0) >= lax.broadcasted_iota(
        jnp.int32, (block_len, block_len), 1
    )
    allowed = causal[None] & (doc_ids[:, :, None] == doc_ids[:, None, :])
    scores = jnp.where(allowed[:, None], scores, 0.0)
    inside = jnp.einsum("nhts,nshe->nthe", scores, values, precision=HIGH)
    in_tail = (doc_ids == doc_ids[:, block_len - 1 :]).astype(decays.dtype)
    ending = key_rows * jnp.exp(final_decay - decays) * in_tail[:, :, None, None]
    states = jnp.einsum("nshc,nshe->nhce", ending, values, precision=HIGH)
    kept_flag = (doc_ids[:, block_len - 1] == before).astype(decays.dtype)
    carried = jnp.exp(final_decay[:, 0]) * kept_flag[:, None, None]
    entering = (doc_ids == before[:, None]).astype(decays.dtype)
    reached = queries * jnp.exp(decays) * entering[:, :, None, None]
    prefix_decay, prefix_state = lax.associative_scan(chain_link, (carried, states), axis=0)
    return (inside, reached, prefix_decay, prefix_state)


def finish(pieces, state_in):
    inside, reached, prefix_decay, prefix_state = pieces
    state_ends = prefix_decay[..., None] * state_in[None] + prefix_state
    state_starts = jnp.concatenate([state_in[None], state_ends[:-1]], axis=0)
    outside = jnp.einsum("nthc,nhce->nthe", reached, state_starts, precision=HIGH)
    summed = inside + outside
    block_count, block_len, head_count, feature = summed.shape
    return (summed.reshape(block_count * block_len, head_count, feature), state_ends[-1])


def body(
    block_in,
    query_proj,
    forget_proj,
    value_proj,
    outgate_proj,
    out_proj,
    ffn_gate,
    ffn_up,
    ffn_down,
    first_gain,
    second_gain,
    group_gain,
    forget_bias,
    bound_table,
    layer_index,
    second_start,
    cotangent,
):
    row_count = block_in.shape[0]
    local_width = query_proj.shape[1]
    head_count = local_width // HEAD
    hidden_width = ffn_gate.shape[1]
    inputs = block_in.astype(jnp.float32)
    first_low = rms_norm(inputs, first_gain).astype(jnp.bfloat16)
    mix_local = jnp.concatenate([query_proj, forget_proj, value_proj, outgate_proj], axis=1)
    ffn_local = jnp.concatenate([ffn_gate, ffn_up], axis=1)
    mix_full, out_full = (
        lax.all_gather(mix_local, "dp", axis=0, tiled=True),
        lax.all_gather(out_proj, "dp", axis=1, tiled=True),
    )
    projected = jnp.dot(first_low, mix_full, preferred_element_type=jnp.float32)
    pre_query = projected[:, :local_width]
    pre_forget = projected[:, local_width : 2 * local_width]
    pre_value = projected[:, 2 * local_width : 3 * local_width]
    pre_outgate = projected[:, 3 * local_width :]
    bound_vec = lower_bound(bound_table, layer_index)
    queries, key_rows, log_forget = gate_values(pre_query, pre_forget, forget_bias, bound_vec)
    offset = lax.axis_index("ctx") * row_count
    doc_ids = (offset + lax.iota(jnp.int32, row_count) >= second_start[0]).astype(jnp.int32)
    prev_doc = (offset - 1 >= second_start[0]).astype(jnp.int32)

    def to_heads(flat):
        return flat.reshape(row_count, head_count, HEAD)

    def mixer(queries_in, keys_in, values_in, logs_in, state_in):
        return finish(
            block_parts(queries_in, keys_in, values_in, logs_in, doc_ids, prev_doc, BLOCK), state_in
        )

    pieces = block_parts(
        to_heads(queries),
        to_heads(key_rows),
        to_heads(pre_value),
        to_heads(log_forget),
        doc_ids,
        prev_doc,
        BLOCK,
    )
    identity = (
        jnp.ones((head_count, HEAD), jnp.float32),
        jnp.zeros((head_count, HEAD, HEAD), jnp.float32),
    )
    shard_decay = pieces[2][-1]
    entry_pair = carried_in((shard_decay, pieces[3][-1]), "ctx", chain_link, identity)
    state_in = entry_pair[1]
    mixed, _ = finish(pieces, state_in)
    mixed_flat = mixed.reshape(row_count, local_width)
    gated_low = head_norm(mixed_flat, pre_outgate, group_gain, head_count).astype(jnp.bfloat16)
    mix_partial = jnp.dot(gated_low, out_full, preferred_element_type=jnp.float32)
    resid = inputs + lax.psum(mix_partial, "tp")
    second_low = rms_norm(resid, second_gain).astype(jnp.bfloat16)
    ffn_full, down_full = (
        lax.all_gather(ffn_local, "dp", axis=0, tiled=True),
        lax.all_gather(ffn_down, "dp", axis=1, tiled=True),
    )
    gate_up = jnp.dot(second_low, ffn_full, preferred_element_type=jnp.float32)
    pre_gate = gate_up[:, :hidden_width]
    pre_up = gate_up[:, hidden_width:]
    hidden_low = (jax.nn.silu(pre_gate) * pre_up).astype(jnp.bfloat16)
    ffn_partial = jnp.dot(hidden_low, down_full, preferred_element_type=jnp.float32)
    block_out = (
        resid + lax.psum(ffn_partial.astype(jnp.bfloat16), "tp").astype(jnp.float32)
    ).astype(jnp.bfloat16)
    mix_full, out_full, ffn_full, down_full = (
        lax.all_gather(mix_local, "dp", axis=0, tiled=True),
        lax.all_gather(out_proj, "dp", axis=1, tiled=True),
        lax.all_gather(ffn_local, "dp", axis=0, tiled=True),
        lax.all_gather(ffn_down, "dp", axis=1, tiled=True),
    )
    cotangent_full = cotangent.astype(jnp.float32)
    hidden_grad = contract_last(cotangent, down_full)
    down_weight_grad = contract_first(hidden_low, cotangent)
    _, act_pull = jax.vjp(lambda gate_in, up_in: jax.nn.silu(gate_in) * up_in, pre_gate, pre_up)
    gate_grad, up_grad = act_pull(hidden_grad)
    gate_up_grad = jnp.concatenate([gate_grad, up_grad], axis=1).astype(jnp.bfloat16)
    second_part = contract_last(gate_up_grad, ffn_full)
    ffn_weight_grad = contract_first(second_low, gate_up_grad)
    second_total = lax.psum(second_part, "tp")
    _, second_pull = jax.vjp(rms_norm, resid, second_gain)
    resid_part, second_gain_grad = second_pull(second_total)
    resid_grad = cotangent_full + resid_part
    resid_low = resid_grad.astype(jnp.bfloat16)
    gated_grad = contract_last(resid_low, out_full)
    out_weight_grad = contract_first(gated_low, resid_low)
    _, head_pull = jax.vjp(
        lambda mixed_in, gate_in, gain_in: head_norm(mixed_in, gate_in, gain_in, head_count),
        mixed_flat,
        pre_outgate,
        group_gain,
    )
    mixed_grad, outgate_pre_grad, group_gain_grad = head_pull(gated_grad)
    _, mixer_pull = jax.vjp(
        mixer,
        to_heads(queries),
        to_heads(key_rows),
        to_heads(pre_value),
        to_heads(log_forget),
        state_in,
    )
    first_pass = mixer_pull(
        (to_heads(mixed_grad), jnp.zeros((head_count, HEAD, HEAD), jnp.float32))
    )
    after_pair = carried_in_2((shard_decay, first_pass[4]), "ctx", chain_link, identity)
    second_pass = mixer_pull((jnp.zeros((row_count, head_count, HEAD), jnp.float32), after_pair[1]))
    query_rec_grad = (first_pass[0] + second_pass[0]).reshape(row_count, local_width)
    key_rec_grad = (first_pass[1] + second_pass[1]).reshape(row_count, local_width)
    value_rec_grad = (first_pass[2] + second_pass[2]).reshape(row_count, local_width)
    log_rec_grad = (first_pass[3] + second_pass[3]).reshape(row_count, local_width)
    _, gate_pull = jax.vjp(gate_values, pre_query, pre_forget, forget_bias, bound_vec)
    query_pre_grad, forget_pre_grad, forget_bias_grad, bound_grad = gate_pull(
        (query_rec_grad, key_rec_grad, log_rec_grad)
    )
    _, table_pull = jax.vjp(lambda rows_in: lower_bound(rows_in, layer_index), bound_table)
    (table_grad,) = table_pull(bound_grad)
    proj_grad = jnp.concatenate(
        [query_pre_grad, forget_pre_grad, value_rec_grad, outgate_pre_grad], axis=1
    ).astype(jnp.bfloat16)
    first_part = contract_last(proj_grad, mix_full)
    mix_weight_grad = contract_first(first_low, proj_grad)
    first_total = lax.psum(first_part.astype(jnp.bfloat16), "tp").astype(jnp.float32)
    _, first_pull = jax.vjp(rms_norm, inputs, first_gain)
    input_part, first_gain_grad = first_pull(first_total)
    input_grad = resid_grad + input_part
    mix_summed, out_summed, ffn_summed, down_summed = (
        lax.psum_scatter(
            mix_weight_grad.astype(jnp.bfloat16), ("dp", "ctx"), scatter_dimension=0, tiled=True
        ).astype(jnp.float32),
        lax.psum_scatter(
            out_weight_grad.astype(jnp.bfloat16), ("dp", "ctx"), scatter_dimension=1, tiled=True
        ).astype(jnp.float32),
        lax.psum_scatter(
            ffn_weight_grad.astype(jnp.bfloat16), ("dp", "ctx"), scatter_dimension=0, tiled=True
        ).astype(jnp.float32),
        lax.psum_scatter(
            down_weight_grad.astype(jnp.bfloat16), ("dp", "ctx"), scatter_dimension=1, tiled=True
        ).astype(jnp.float32),
    )
    mix_shard, out_shard, ffn_shard, down_shard = (
        lax.all_gather(mix_summed.astype(jnp.bfloat16), "ctx", axis=0, tiled=True).astype(
            mix_summed.dtype
        ),
        lax.all_gather(out_summed.astype(jnp.bfloat16), "ctx", axis=1, tiled=True).astype(
            out_summed.dtype
        ),
        lax.all_gather(ffn_summed.astype(jnp.bfloat16), "ctx", axis=0, tiled=True).astype(
            ffn_summed.dtype
        ),
        lax.all_gather(down_summed.astype(jnp.bfloat16), "ctx", axis=1, tiled=True).astype(
            down_summed.dtype
        ),
    )
    first_sum, second_sum, group_sum, bias_sum, table_sum = (
        lax.psum(first_gain_grad.astype(jnp.bfloat16), ("dp", "ctx")).astype(jnp.float32),
        lax.psum(second_gain_grad.astype(jnp.bfloat16), ("dp", "ctx")).astype(jnp.float32),
        lax.psum(group_gain_grad.astype(jnp.bfloat16), ("dp", "ctx")).astype(jnp.float32),
        lax.psum(forget_bias_grad.astype(jnp.bfloat16), ("dp", "ctx")).astype(jnp.float32),
        lax.psum(table_grad.astype(jnp.bfloat16), ("dp", "ctx")).astype(jnp.float32),
    )
    return (
        block_out,
        input_grad,
        mix_shard[:, :local_width],
        mix_shard[:, local_width : 2 * local_width],
        mix_shard[:, 2 * local_width : 3 * local_width],
        mix_shard[:, 3 * local_width :],
        out_shard,
        ffn_shard[:, :hidden_width],
        ffn_shard[:, hidden_width:],
        down_shard,
        first_sum,
        second_sum,
        group_sum,
        bias_sum,
        table_sum,
    )


def solution(mesh):
    return jax.shard_map(
        body,
        mesh=mesh,
        in_specs=(
            P(("dp", "ctx"), None),
            P("dp", "tp"),
            P("dp", "tp"),
            P("dp", "tp"),
            P("dp", "tp"),
            P("tp", "dp"),
            P("dp", "tp"),
            P("dp", "tp"),
            P("tp", "dp"),
            P(),
            P(),
            P("tp"),
            P("tp"),
            P(None, "tp"),
            P(),
            P("dp"),
            P(("dp", "ctx"), None),
        ),
        out_specs=(
            P(("dp", "ctx"), None),
            P(("dp", "ctx"), None),
            P("dp", "tp"),
            P("dp", "tp"),
            P("dp", "tp"),
            P("dp", "tp"),
            P("tp", "dp"),
            P("dp", "tp"),
            P("dp", "tp"),
            P("tp", "dp"),
            P(),
            P(),
            P("tp"),
            P("tp"),
            P(None, "tp"),
        ),
        check_vma=False,
    )
```

profile of v0, /device:TPU:0, one launch (start us, length us, event | category | flops | bytes accessed | tf_op | source)
XLA Modules:
  0.0 2218.8 jit_solution(17821822070272523341)
XLA Ops:
  17.0 145.9 %all-gather.8.cloned.1.call-done = bf16[2048,2048]{1,0:T(8,128)(2,1)} async-done(((bf16[512,2048]{1,0:T(8,128)(2,1)}), bf16[2048,2048]{1,0:T(8,128)(2,1)}) %all-gather.8.cloned.1.call-update) | async-done | bytes 8388624 | tf_op jit(solution)/shard_map/all_gather | solution.py:170
  268.4 18.6 pad.557
  312.1 35.5 %pad.734 = f32[31,4,128,128]{2,3,1,0:T(8,128)} pad(f32[16,4,128,128]{2,3,1,0:T(8,128)} %pad_maximum_fusion.5, f32[]{:T(128)} %constant.113.clone.1), padding=0_0_1x0_0_0x0_0_0x0_0_0 | pad | bytes 12320772 | tf_op jit(solution)/shard_map/slice | solution.py:135
  347.6 35.6 %pad.559 = f32[32,4,128,128]{2,3,1,0:T(8,128)} pad(f32[16,4,128,128]{2,3,1,0:T(8,128)} %pad_maximum_fusion.5, f32[]{:T(128)} %constant.113.clone.1), padding=0_1_1x0_0_0x0_0_0x0_0_0 | pad | bytes 12582916 | tf_op jit(solution)/shard_map/pad | solution.py:128
  385.0 35.6 %pad.1005 = f32[32,4,128,128]{2,3,1,0:T(8,128)} pad(f32[16,4,128,128]{2,3,1,0:T(8,128)} %add.591, f32[]{:T(128)} %constant.113.clone.1), padding=1_0_1x0_0_0x0_0_0x0_0_0 | pad | bytes 12582916
  499.8 166.2 %all-reduce.122.cloned.1.call-done = f32[1024,2048]{1,0:T(8,128)} async-done(((f32[1024,2048]{1,0:T(8,128)}), f32[1024,2048]{1,0:T(8,128)}) %all-reduce.122.cloned.1.call-update) | async-done | bytes 8388624 | tf_op jit(solution)/shard_map/psum | solution.py:212
  675.0 194.9 %all-gather.12.cloned.1.call-done = bf16[2048,2816]{1,0:T(8,128)(2,1)} async-done(((bf16[512,2816]{1,0:T(8,128)(2,1)}), bf16[2048,2816]{1,0:T(8,128)(2,1)}) %all-gather.12.cloned.1.call-update) | async-done | bytes 11534352 | tf_op jit(solution)/shard_map/all_gather | solution.py:215
  869.9 20.0 fusion.177
  889.9 86.4 %all-gather.14.cloned.1.call-done = bf16[1408,2048]{1,0:T(8,128)(2,1)} async-done(((bf16[1408,512]{1,0:T(8,128)(2,1)}), bf16[1408,2048]{1,0:T(8,128)(2,1)}) %all-gather.14.cloned.1.call-update) | async-done | bytes 5767184 | tf_op jit(solution)/shard_map/all_gather | solution.py:216
  995.1 16.8 fusion.20
  1054.8 18.7 convolution_convert_fusion
  1084.6 97.8 %all-reduce.124.cloned.1.call-done = f32[1024,2048]{1,0:T(8,128)} async-done(((f32[1024,2048]{1,0:T(8,128)}), f32[1024,2048]{1,0:T(8,128)}) %all-reduce.124.cloned.1.call-update) | async-done | bytes 8388624 | tf_op jit(solution)/shard_map/psum | solution.py:240
  1413.1 18.5 pad.623
  1435.8 18.6 pad.624
  1510.5 35.6 %pad.625 = f32[32,4,128,128]{2,3,1,0:T(8,128)} pad(f32[16,4,128,128]{2,3,1,0:T(8,128)} %get-tuple-element.256, f32[]{:T(128)} %constant.113.clone.1), padding=1_0_1x0_0_0x0_0_0x0_0_0 | pad | bytes 12582916 | tf_op jit(solution)/shard_map/transpose(jvp())/pad | solution.py:128
  1546.0 35.5 %pad.591 = f32[32,4,128,128]{2,3,1,0:T(8,128)} pad(f32[16,4,128,128]{2,3,1,0:T(8,128)} %get-tuple-element.255, f32[]{:T(128)} %constant.113.clone.1), padding=1_0_1x0_0_0x0_0_0x0_0_0 | pad | bytes 12582916 | tf_op jit(solution)/shard_map/transpose(jvp())/pad | solution.py:128
  1590.3 35.6 %pad.592 = f32[32,4,128,128]{2,3,1,0:T(8,128)} pad(f32[16,4,128,128]{2,3,1,0:T(8,128)} %get-tuple-element.375, f32[]{:T(128)} %constant.113.clone.1), padding=0_1_1x0_0_0x0_0_0x0_0_0 | pad | bytes 12582916 | tf_op jit(solution)/shard_map/transpose(jvp())/pad | solution.py:128
  1625.9 35.7 %pad.626 = f32[32,4,128,128]{2,3,1,0:T(8,128)} pad(f32[16,4,128,128]{2,3,1,0:T(8,128)} %get-tuple-element.376, f32[]{:T(128)} %constant.113.clone.1), padding=0_1_1x0_0_0x0_0_0x0_0_0 | pad | bytes 12582916 | tf_op jit(solution)/shard_map/transpose(jvp())/pad | solution.py:128
  1661.7 33.6 %pad.562 = f32[32,4,128,128]{2,3,1,0:T(8,128)} pad(f32[15,4,128,128]{2,3,1,0:T(8,128)} %get-tuple-element.290, f32[]{:T(128)} %constant.113.clone.1), padding=2_1_1x0_0_0x0_0_0x0_0_0 | pad | bytes 12320772 | tf_op jit(solution)/shard_map/transpose(jvp())/pad | solution.py:128
  1695.3 33.7 %pad.597 = f32[32,4,128,128]{2,3,1,0:T(8,128)} pad(f32[15,4,128,128]{2,3,1,0:T(8,128)} %get-tuple-element.291, f32[]{:T(128)} %constant.113.clone.1), padding=2_1_1x0_0_0x0_0_0x0_0_0 | pad | bytes 12320772 | tf_op jit(solution)/shard_map/transpose(jvp())/pad | solution.py:128
  1810.3 19.3 fusion.176
  1913.4 152.0 %all-reduce.126.cloned.1.call-done = (bf16[1024,2048]{1,0:T(8,128)(2,1)}, bf16[1024,2048]{1,0:T(8,128)(2,1)}) async-done(((bf16[1024,2048]{1,0:T(8,128)(2,1)}, bf16[1024,2048]{1,0:T(8,128)(2,1)}), (bf16[1024,2048]{1,0:T(8,128)(2,1)}, bf16[1024,2048]{1,0:T(8,128)(2,1)})) %all-reduce.126.cloned.1.call-update) | async-done | bytes 8388624 | tf_op jit(solution)/shard_map/psum | solution.py:224
  2073.8 84.8 %reduce-scatter.5.cloned.1.call-done = bf16[256,2048]{1,0:T(8,128)(2,1)} async-done(((bf16[2048,2048]{1,0:T(8,128)(2,1)}), bf16[256,2048]{1,0:T(8,128)(2,1)}) %reduce-scatter.5.cloned.1.call-update) | async-done | bytes 1048592 | tf_op jit(solution)/shard_map/reduce_scatter | solution.py:287
  2164.6 26.3 %all-reduce.116 = (bf16[2048]{0:T(1024)(128)(2,1)S(1)}, bf16[2048]{0:T(1024)(128)(2,1)S(1)}, bf16[512]{0:T(512)(128)(2,1)S(1)}, bf16[512]{0:T(512)(128)(2,1)S(1)}, bf16[24,512]{1,0:T(8,128)(2,1)S(1)}) all-reduce(bf16[2048]{0:T(1024)(128)(2,1)S(1)} %get-tuple-element.200, ...), channel_id=1, replica_groups=mesh['dp'=4,'ctx'=2,'tp'=4] {'dp','ctx'}, use_global_device_ids=true, to_apply=%region_51.52 | all-reduce | flops 17408 | bytes 69632 | tf_op jit(solution)/shard_map/psum | solution.py:315
  (832 shorter events, 799.1 us)
Async XLA Ops:
  7.2 155.7 %all-gather.8.cloned.1.call-start = ((), (), s32[]{:S(2)}) async-start(), calls=%async_computation.4 | async-start | bytes 10485760 | tf_op jit(solution)/shard_map/all_gather | solution.py:170
  10.4 477.5 %all-gather.10.cloned.1.call-start = ((), (), s32[]{:S(2)}) async-start(), calls=%async_computation.5 | async-start | bytes 2621440 | tf_op jit(solution)/shard_map/all_gather | solution.py:171
  11.1 654.9 %all-reduce.122.cloned.1.call-start = ((), (), s32[]{:S(2)}) async-start(), calls=%async_computation.6 | async-start | bytes 16777216 | tf_op jit(solution)/shard_map/psum | solution.py:212
  16.4 159.0 %copy-start.171 = (f32[1024]{0:T(1024)}, f32[1024]{0:T(1024)S(1)}, u32[]{:S(2)}) copy-start(f32[1024]{0:T(1024)S(1)} %fusion.149) | copy-start | bytes 12292
  16.6 158.8 %copy-start.178 = (f32[512]{0:T(512)}, f32[512]{0:T(512)S(1)}, u32[]{:S(2)}) copy-start(f32[512]{0:T(512)S(1)} %multiply_reduce_fusion.28) | copy-start | bytes 6148
  16.6 158.8 %copy-start.196 = (f32[512]{0:T(512)}, f32[512]{0:T(512)S(1)}, u32[]{:S(2)}) copy-start(f32[512]{0:T(512)S(1)} %broadcast_subtract_fusion) | copy-start | bytes 6148
  16.7 169.4 %copy-start.214 = (f32[32]{0:T(128)}, f32[32]{0:T(128)S(1)}, u32[]{:S(2)}) copy-start(f32[32]{0:T(128)S(1)} %get-tuple-element.269) | copy-start | bytes 388
  16.9 1024.1 %copy-start.73 = (pred[32,32,32]{2,1,0:T(8,128)(4,1)}, pred[32,32,32]{2,1,0:T(8,128)(4,1)S(1)}, u32[]{:S(2)}) copy-start(pred[32,32,32]{2,1,0:T(8,128)(4,1)S(1)} %compare_and_fusion) | copy-start | bytes 98308
  16.9 189.3 %copy-start.131 = (f32[32,32]{0,1:T(8,128)}, f32[32,32]{0,1:T(8,128)S(1)}, u32[]{:S(2)}) copy-start(f32[32,32]{0,1:T(8,128)S(1)} %get-tuple-element.440) | copy-start | bytes 12292
  16.9 415.8 %copy-start.129 = (f32[32,32]{0,1:T(8,128)}, f32[32,32]{0,1:T(8,128)S(1)}, u32[]{:S(2)}) copy-start(f32[32,32]{0,1:T(8,128)S(1)} %get-tuple-element.439) | copy-start | bytes 12292
  17.0 158.5 %copy-start.204 = (f32[512]{0:T(512)S(1)}, f32[512]{0:T(512)}, u32[]{:S(2)}) copy-start(f32[512]{0:T(512)} %param.31) | copy-start | bytes 6148
  424.2 600.7 %copy-start.88 = (f32[1,4,128,128]{2,3,1,0:T(8,128)}, f32[1,4,128,128]{2,3,1,0:T(8,128)S(1)}, u32[]{:S(2)}) copy-start(f32[1,4,128,128]{2,3,1,0:T(8,128)S(1)} %add_select_fusion) | copy-start | bytes 786436
  495.5 374.3 %all-gather.12.cloned.1.call-start = ((), (), s32[]{:S(2)}) async-start(), calls=%async_computation.7 | async-start | bytes 14417920 | tf_op jit(solution)/shard_map/all_gather | solution.py:215
  499.2 477.1 %all-gather.14.cloned.1.call-start = ((), (), s32[]{:S(2)}) async-start(), calls=%async_computation.8 | async-start | bytes 7208960 | tf_op jit(solution)/shard_map/all_gather | solution.py:216
  499.7 370.1 %copy-start.177 = (f32[2048]{0:T(1024)S(1)}, f32[2048]{0:T(1024)}, u32[]{:S(2)}) copy-start(f32[2048]{0:T(1024)} %param.29) | copy-start | bytes 24580
  499.8 682.7 %all-reduce.124.cloned.1.call-start = ((), (), s32[]{:S(2)}) async-start(), calls=%async_computation.9 | async-start | bytes 16777216 | tf_op jit(solution)/shard_map/psum | solution.py:240
  1011.9 865.1 %reduce-scatter.11.cloned.1.call-start = ((), (), s32[]{:S(2)}) async-start(), calls=%async_computation.15 | async-start | bytes 6488064 | tf_op jit(solution)/shard_map/reduce_scatter | solution.py:296
  1022.5 882.9 %reduce-scatter.9.cloned.1.call-start = ((), (), s32[]{:S(2)}) async-start(), calls=%async_computation.13 | async-start | bytes 12976128 | tf_op jit(solution)/shard_map/reduce_scatter | solution.py:293
  1073.5 833.1 %reduce-scatter.7.cloned.1.call-start = ((), (), s32[]{:S(2)}) async-start(), calls=%async_computation.12 | async-start | bytes 2359296 | tf_op jit(solution)/shard_map/reduce_scatter | solution.py:290
  1808.8 101.3 %all-gather.20.cloned.1.call-start = ((), (), s32[]{:S(2)}) async-start(), calls=%async_computation.16 | async-start | bytes 2162688 | tf_op jit(solution)/shard_map/all_gather | solution.py:310
  1877.1 188.4 %all-reduce.126.cloned.1.call-start = ((), (), s32[]{:S(2)}) async-start(), calls=%async_computation.17 | async-start | bytes 16777216 | tf_op jit(solution)/shard_map/psum | solution.py:224
  1890.0 268.6 %reduce-scatter.5.cloned.1.call-start = ((), (), s32[]{:S(2)}) async-start(), calls=%async_computation.10 | async-start | bytes 9437184 | tf_op jit(solution)/shard_map/reduce_scatter | solution.py:287
  1905.3 298.1 %all-gather.18.cloned.1.call-start = ((), (), s32[]{:S(2)}) async-start(), calls=%async_computation.14 | async-start | bytes 4325376 | tf_op jit(solution)/shard_map/all_gather | solution.py:307
  1906.0 302.0 %all-gather.16.cloned.1.call-start = ((), (), s32[]{:S(2)}) async-start(), calls=%async_computation.11 | async-start | bytes 3145728 | tf_op jit(solution)/shard_map/all_gather | solution.py:301
  (237 other events, 2089.7 us)
Sparse Core Ops, SparseCore 0:
  10.5 152.3 all-gather.7
  164.4 44.1 all-gather.9
  495.6 170.3 all-reduce.121
  668.1 201.7 all-gather.11
  871.3 104.8 all-gather.13
  1012.0 170.3 all-reduce.123
  1184.7 65.5 reduce-scatter.10
  1252.6 117.6 reduce-scatter.8
  1808.8 36.2 reduce-scatter.6
  1877.2 10.0 all-gather.19
  1891.6 173.7 all-reduce.125
  2068.3 90.2 reduce-scatter.4
  2160.2 10.1 all-gather.17
  2171.8 11.7 all-gather.15
where the time goes:
time: 2250 us; the launch traced here: 2220 us
  waiting for transfers between devices  930 us (41%)
  local copies, waits for them, and re-layouts  640 us (28%)
  matrix products  319 us (14%)
  other arithmetic  275 us (12%)
  blocking collectives  36.4 us (2%)
    pad x74, local copies, waits for them, and re-layouts, block_parts(): lax.associative_scan(chain_link, (carried, states), axis=0)  483 us
    all_gather x1, waiting for transfers between devices, body(): lax.all_gather(ffn_local, 'dp', axis=0, tiled=True)  195 us
    psum x1, waiting for transfers between devices, body(): resid = inputs + lax.psum(mix_partial, 'tp')  166 us
    psum x1, waiting for transfers between devices, body(): lax.psum(ffn_partial.astype(jnp.bfloat16), 'tp').astype(jnp.float32)  152 us
    all_gather x1, waiting for transfers between devices, body(): lax.all_gather(mix_local, 'dp', axis=0, tiled=True)  146 us
    psum x1, waiting for transfers between devices, body(): second_total = lax.psum(second_part, 'tp')  97.8 us
    all_gather x1, waiting for transfers between devices, body(): lax.all_gather(ffn_down, 'dp', axis=1, tiled=True)  86.4 us
    reduce_scatter x1, waiting for transfers between devices, body(): lax.psum_scatter(mix_weight_grad.astype(jnp.bfloat16), ('dp', 'ctx'), sca...  84.8 us
  transfers between devices with their start and end apart: 14, of which 7 were waited for; matrix products, arithmetic and copies ran while one was open for 51% of the time, Pallas kernels for 0%

commit v1 on v0

--- a/solution.py
+++ b/solution.py
@@ -221,7 +221,10 @@
     hidden_low = (jax.nn.silu(pre_gate) * pre_up).astype(jnp.bfloat16)
     ffn_partial = jnp.dot(hidden_low, down_full, preferred_element_type=jnp.float32)
     block_out = (
-        resid + lax.psum(ffn_partial.astype(jnp.bfloat16), "tp").astype(jnp.float32)
+        resid
+        + jnp.sum(lax.all_gather(ffn_partial.astype(jnp.bfloat16), "tp"), axis=0).astype(
+            jnp.float32
+        )
     ).astype(jnp.bfloat16)
     mix_full, out_full, ffn_full, down_full = (
         lax.all_gather(mix_local, "dp", axis=0, tiled=True),

time: 2250 us -> 2530 us (1.12)
  waiting for transfers between devices: 930 us -> 1220 us
  local copies, waits for them, and re-layouts: 640 us -> 603 us
    all_gather x0 -> x1, waiting for transfers between devices: none -> 158 us  [body(): lax.all_gather(ffn_partial.astype(jnp.bfloat16), 'tp')]
    reduce_scatter x1, waiting for transfers between devices: 0.02 us -> 115 us  [body(): lax.psum_scatter(ffn_weight_grad.astype(jnp.bfloat16), ('dp', 'ctx'), sca...]
    psum x1, waiting for transfers between devices: 97.8 us -> 154 us  [body(): second_total = lax.psum(second_part, 'tp')]
    psum x1, waiting for transfers between devices: 152 us -> 102 us  [body(): lax.psum(first_part.astype(jnp.bfloat16), 'tp').astype(jnp.float32)]
    reduce_scatter x1, waiting for transfers between devices: 0.02 us -> 36.4 us  [body(): lax.psum_scatter(out_weight_grad.astype(jnp.bfloat16), ('dp', 'ctx'), sca...]
    pad x74, local copies, waits for them, and re-layouts: 483 us -> 455 us  [block_parts(): lax.associative_scan(chain_link, (carried, states), axis=0)]
    reduce_scatter x1, waiting for transfers between devices: 84.8 us -> 57.9 us  [body(): lax.psum_scatter(mix_weight_grad.astype(jnp.bfloat16), ('dp', 'ctx'), sca...]
    unnamed x468 -> x406, local copies, waits for them, and re-layouts: 79.2 us -> 70.8 us
  transfers between devices with their start and end apart: 14 -> 15, of which waited for: 7 -> 10; matrix products, arithmetic and copies ran while one was open for 51% -> 46% of each run, Pallas kernels for 0% -> 0%
where the time goes in v1:
time: 2530 us; the launch traced here: 2490 us
  waiting for transfers between devices  1220 us (48%)
  local copies, waits for them, and re-layouts  603 us (24%)
  matrix products  325 us (13%)
  other arithmetic  288 us (11%)
  blocking collectives  39 us (2%)
    pad x74, local copies, waits for them, and re-layouts, block_parts(): lax.associative_scan(chain_link, (carried, states), axis=0)  455 us
    all_gather x1, waiting for transfers between devices, body(): lax.all_gather(ffn_local, 'dp', axis=0, tiled=True)  195 us
    psum x1, waiting for transfers between devices, body(): resid = inputs + lax.psum(mix_partial, 'tp')  166 us
    all_gather x1, waiting for transfers between devices, body(): lax.all_gather(ffn_partial.astype(jnp.bfloat16), 'tp')  158 us
    psum x1, waiting for transfers between devices, body(): second_total = lax.psum(second_part, 'tp')  154 us
    all_gather x1, waiting for transfers between devices, body(): lax.all_gather(mix_local, 'dp', axis=0, tiled=True)  146 us
    reduce_scatter x1, waiting for transfers between devices, body(): lax.psum_scatter(ffn_weight_grad.astype(jnp.bfloat16), ('dp', 'ctx'), sca...  115 us
    psum x1, waiting for transfers between devices, body(): lax.psum(first_part.astype(jnp.bfloat16), 'tp').astype(jnp.float32)  102 us
  transfers between devices with their start and end apart: 15, of which 10 were waited for; matrix products, arithmetic and copies ran while one was open for 46% of the time, Pallas kernels for 0%

profile of v1, /device:TPU:0, one launch (start us, length us, event | category | flops | bytes accessed | tf_op | source)
XLA Modules:
  0.0 2493.0 jit_solution(4363003864523052526)
XLA Ops:
  17.0 145.9 %all-gather.10.cloned.1.call-done = bf16[2048,2048]{1,0:T(8,128)(2,1)} async-done(((bf16[512,2048]{1,0:T(8,128)(2,1)}), bf16[2048,2048]{1,0:T(8,128)(2,1)}) %all-gather.10.cloned.1.call-update) | async-done | bytes 8388624 | tf_op jit(solution)/shard_map/all_gather | solution.py:170
  312.0 35.4 %pad.734 = f32[31,4,128,128]{2,3,1,0:T(8,128)} pad(f32[16,4,128,128]{2,3,1,0:T(8,128)} %pad_maximum_fusion.5, f32[]{:T(128)} %constant.114.clone.1), padding=0_0_1x0_0_0x0_0_0x0_0_0 | pad | bytes 12320772 | tf_op jit(solution)/shard_map/slice | solution.py:135
  347.4 35.5 %pad.559 = f32[32,4,128,128]{2,3,1,0:T(8,128)} pad(f32[16,4,128,128]{2,3,1,0:T(8,128)} %pad_maximum_fusion.5, f32[]{:T(128)} %constant.114.clone.1), padding=0_1_1x0_0_0x0_0_0x0_0_0 | pad | bytes 12582916 | tf_op jit(solution)/shard_map/pad | solution.py:128
  384.7 35.6 %pad.1005 = f32[32,4,128,128]{2,3,1,0:T(8,128)} pad(f32[16,4,128,128]{2,3,1,0:T(8,128)} %add.589, f32[]{:T(128)} %constant.114.clone.1), padding=1_0_1x0_0_0x0_0_0x0_0_0 | pad | bytes 12582916
  499.1 166.2 %all-reduce.121.cloned.1.call-done = f32[1024,2048]{1,0:T(8,128)} async-done(((f32[1024,2048]{1,0:T(8,128)}), f32[1024,2048]{1,0:T(8,128)}) %all-reduce.121.cloned.1.call-update) | async-done | bytes 8388624 | tf_op jit(solution)/shard_map/psum | solution.py:212
  674.2 194.9 %all-gather.14.cloned.1.call-done = bf16[2048,2816]{1,0:T(8,128)(2,1)} async-done(((bf16[512,2816]{1,0:T(8,128)(2,1)}), bf16[2048,2816]{1,0:T(8,128)(2,1)}) %all-gather.14.cloned.1.call-update) | async-done | bytes 11534352 | tf_op jit(solution)/shard_map/all_gather | solution.py:215
  869.1 20.0 fusion.177
  889.1 86.4 %all-gather.16.cloned.1.call-done = bf16[1408,2048]{1,0:T(8,128)(2,1)} async-done(((bf16[1408,512]{1,0:T(8,128)(2,1)}), bf16[1408,2048]{1,0:T(8,128)(2,1)}) %all-gather.16.cloned.1.call-update) | async-done | bytes 5767184 | tf_op jit(solution)/shard_map/all_gather | solution.py:216
  1002.2 19.4 fusion.20
  1021.7 19.4 convolution_convert_fusion
  1085.8 154.1 %all-reduce.123.cloned.1.call-done = f32[1024,2048]{1,0:T(8,128)} async-done(((f32[1024,2048]{1,0:T(8,128)}), f32[1024,2048]{1,0:T(8,128)}) %all-reduce.123.cloned.1.call-update) | async-done | bytes 8388624 | tf_op jit(solution)/shard_map/psum | solution.py:243
  1247.5 114.7 %reduce-scatter.9.cloned.1.call-done = bf16[256,2816]{1,0:T(8,128)(2,1)} async-done(((bf16[2048,2816]{1,0:T(8,128)(2,1)}), bf16[256,2816]{1,0:T(8,128)(2,1)}) %reduce-scatter.9.cloned.1.call-update) | async-done | bytes 1441808 | tf_op jit(solution)/shard_map/reduce_scatter | solution.py:296
  1362.3 158.2 %all-gather.24.cloned.1.call-done = bf16[4096,2048]{1,0:T(8,128)(2,1)} async-done(((bf16[1024,2048]{1,0:T(8,128)(2,1)}), bf16[4096,2048]{1,0:T(8,128)(2,1)}) %all-gather.24.cloned.1.call-update) | async-done | bytes 16777232 | tf_op jit(solution)/shard_map/all_gather | solution.py:225
  1847.4 35.5 %pad.625 = f32[32,4,128,128]{2,3,1,0:T(8,128)} pad(f32[16,4,128,128]{2,3,1,0:T(8,128)} %get-tuple-element.254, f32[]{:T(128)} %constant.114.clone.1), padding=1_0_1x0_0_0x0_0_0x0_0_0 | pad | bytes 12582916 | tf_op jit(solution)/shard_map/transpose(jvp())/pad | solution.py:128
  1891.6 35.6 %pad.591 = f32[32,4,128,128]{2,3,1,0:T(8,128)} pad(f32[16,4,128,128]{2,3,1,0:T(8,128)} %get-tuple-element.253, f32[]{:T(128)} %constant.114.clone.1), padding=1_0_1x0_0_0x0_0_0x0_0_0 | pad | bytes 12582916 | tf_op jit(solution)/shard_map/transpose(jvp())/pad | solution.py:128
  1927.2 35.7 %pad.592 = f32[32,4,128,128]{2,3,1,0:T(8,128)} pad(f32[16,4,128,128]{2,3,1,0:T(8,128)} %get-tuple-element.375, f32[]{:T(128)} %constant.114.clone.1), padding=0_1_1x0_0_0x0_0_0x0_0_0 | pad | bytes 12582916 | tf_op jit(solution)/shard_map/transpose(jvp())/pad | solution.py:128
  1962.9 33.5 %pad.562 = f32[32,4,128,128]{2,3,1,0:T(8,128)} pad(f32[15,4,128,128]{2,3,1,0:T(8,128)} %get-tuple-element.290, f32[]{:T(128)} %constant.114.clone.1), padding=2_1_1x0_0_0x0_0_0x0_0_0 | pad | bytes 12320772 | tf_op jit(solution)/shard_map/transpose(jvp())/pad | solution.py:128
  2030.2 35.7 %pad.626 = f32[32,4,128,128]{2,3,1,0:T(8,128)} pad(f32[16,4,128,128]{2,3,1,0:T(8,128)} %get-tuple-element.376, f32[]{:T(128)} %constant.114.clone.1), padding=0_1_1x0_0_0x0_0_0x0_0_0 | pad | bytes 12582916 | tf_op jit(solution)/shard_map/transpose(jvp())/pad | solution.py:128
  2066.0 33.6 %pad.597 = f32[32,4,128,128]{2,3,1,0:T(8,128)} pad(f32[15,4,128,128]{2,3,1,0:T(8,128)} %get-tuple-element.291, f32[]{:T(128)} %constant.114.clone.1), padding=2_1_1x0_0_0x0_0_0x0_0_0 | pad | bytes 12320772 | tf_op jit(solution)/shard_map/transpose(jvp())/pad | solution.py:128
  2136.5 19.2 fusion.176
  2234.6 57.9 %reduce-scatter.5.cloned.1.call-done = bf16[256,2048]{1,0:T(8,128)(2,1)} async-done(((bf16[2048,2048]{1,0:T(8,128)(2,1)}), bf16[256,2048]{1,0:T(8,128)(2,1)}) %reduce-scatter.5.cloned.1.call-update) | async-done | bytes 1048592 | tf_op jit(solution)/shard_map/reduce_scatter | solution.py:290
  2292.6 36.4 %reduce-scatter.7.cloned.1.call-done = bf16[512,256]{1,0:T(8,128)(2,1)} async-done(((bf16[512,2048]{1,0:T(8,128)(2,1)}), bf16[512,256]{1,0:T(8,128)(2,1)}) %reduce-scatter.7.cloned.1.call-update) | async-done | bytes 262160 | tf_op jit(solution)/shard_map/reduce_scatter | solution.py:293
  2332.5 102.2 %all-reduce.125.cloned.1.call-done = bf16[1024,2048]{1,0:T(8,128)(2,1)} async-done(((bf16[1024,2048]{1,0:T(8,128)(2,1)}), bf16[1024,2048]{1,0:T(8,128)(2,1)}) %all-reduce.125.cloned.1.call-update) | async-done | bytes 4194320 | tf_op jit(solution)/shard_map/psum | solution.py:285
  2440.8 28.9 %all-reduce.116 = (bf16[2048]{0:T(1024)(128)(2,1)S(1)}, bf16[2048]{0:T(1024)(128)(2,1)S(1)}, bf16[512]{0:T(512)(128)(2,1)S(1)}, bf16[512]{0:T(512)(128)(2,1)S(1)}, bf16[24,512]{1,0:T(8,128)(2,1)S(1)}) all-reduce(bf16[2048]{0:T(1024)(128)(2,1)S(1)} %get-tuple-element.200, ...), channel_id=1, replica_groups=mesh['dp'=4,'ctx'=2,'tp'=4] {'dp','ctx'}, use_global_device_ids=true, to_apply=%region_51.52 | all-reduce | flops 17408 | bytes 69632 | tf_op jit(solution)/shard_map/psum | solution.py:318
  (764 shorter events, 834.8 us)
Async XLA Ops:
  7.2 155.7 %all-gather.10.cloned.1.call-start = ((), (), s32[]{:S(2)}) async-start(), calls=%async_computation.4 | async-start | bytes 10485760 | tf_op jit(solution)/shard_map/all_gather | solution.py:170
  10.4 476.8 %all-gather.12.cloned.1.call-start = ((), (), s32[]{:S(2)}) async-start(), calls=%async_computation.5 | async-start | bytes 2621440 | tf_op jit(solution)/shard_map/all_gather | solution.py:171
  11.1 654.2 %all-reduce.121.cloned.1.call-start = ((), (), s32[]{:S(2)}) async-start(), calls=%async_computation.6 | async-start | bytes 16777216 | tf_op jit(solution)/shard_map/psum | solution.py:212
  16.4 159.0 %copy-start.163 = (f32[1024]{0:T(1024)}, f32[1024]{0:T(1024)S(1)}, u32[]{:S(2)}) copy-start(f32[1024]{0:T(1024)S(1)} %fusion.149) | copy-start | bytes 12292
  16.6 158.8 %copy-start.165 = (f32[512]{0:T(512)}, f32[512]{0:T(512)S(1)}, u32[]{:S(2)}) copy-start(f32[512]{0:T(512)S(1)} %multiply_reduce_fusion.28) | copy-start | bytes 6148
  16.6 158.8 %copy-start.176 = (f32[512]{0:T(512)}, f32[512]{0:T(512)S(1)}, u32[]{:S(2)}) copy-start(f32[512]{0:T(512)S(1)} %broadcast_subtract_fusion) | copy-start | bytes 6148
  16.7 169.4 %copy-start.190 = (f32[32]{0:T(128)}, f32[32]{0:T(128)S(1)}, u32[]{:S(2)}) copy-start(f32[32]{0:T(128)S(1)} %get-tuple-element.267) | copy-start | bytes 388
  16.9 1563.9 %copy-start.69 = (pred[32,32,32]{2,1,0:T(8,128)(4,1)}, pred[32,32,32]{2,1,0:T(8,128)(4,1)S(1)}, u32[]{:S(2)}) copy-start(pred[32,32,32]{2,1,0:T(8,128)(4,1)S(1)} %compare_and_fusion) | copy-start | bytes 98308
  16.9 189.3 %copy-start.132 = (f32[32,32]{0,1:T(8,128)}, f32[32,32]{0,1:T(8,128)S(1)}, u32[]{:S(2)}) copy-start(f32[32,32]{0,1:T(8,128)S(1)} %get-tuple-element.440) | copy-start | bytes 12292
  16.9 415.5 %copy-start.130 = (f32[32,32]{0,1:T(8,128)}, f32[32,32]{0,1:T(8,128)S(1)}, u32[]{:S(2)}) copy-start(f32[32,32]{0,1:T(8,128)S(1)} %get-tuple-element.439) | copy-start | bytes 12292
  17.0 158.5 %copy-start.182 = (f32[512]{0:T(512)S(1)}, f32[512]{0:T(512)}, u32[]{:S(2)}) copy-start(f32[512]{0:T(512)} %param.31) | copy-start | bytes 6148
  494.8 374.3 %all-gather.14.cloned.1.call-start = ((), (), s32[]{:S(2)}) async-start(), calls=%async_computation.7 | async-start | bytes 14417920 | tf_op jit(solution)/shard_map/all_gather | solution.py:215
  498.4 477.1 %all-gather.16.cloned.1.call-start = ((), (), s32[]{:S(2)}) async-start(), calls=%async_computation.8 | async-start | bytes 7208960 | tf_op jit(solution)/shard_map/all_gather | solution.py:216
  499.0 370.1 %copy-start.175 = (f32[2048]{0:T(1024)S(1)}, f32[2048]{0:T(1024)}, u32[]{:S(2)}) copy-start(f32[2048]{0:T(1024)} %param.29) | copy-start | bytes 24580
  499.0 579.9 %reduce-scatter.11.cloned.1.call-start = ((), (), s32[]{:S(2)}) async-start(), calls=%async_computation.16 | async-start | bytes 6488064 | tf_op jit(solution)/shard_map/reduce_scatter | solution.py:299
  1002.1 237.7 %all-reduce.123.cloned.1.call-start = ((), (), s32[]{:S(2)}) async-start(), calls=%async_computation.9 | async-start | bytes 16777216 | tf_op jit(solution)/shard_map/psum | solution.py:243
  1021.7 340.6 %reduce-scatter.9.cloned.1.call-start = ((), (), s32[]{:S(2)}) async-start(), calls=%async_computation.14 | async-start | bytes 12976128 | tf_op jit(solution)/shard_map/reduce_scatter | solution.py:296
  1041.1 479.3 %all-gather.24.cloned.1.call-start = ((), (), s32[]{:S(2)}) async-start(), calls=%async_computation.18 | async-start | bytes 20971520 | tf_op jit(solution)/shard_map/all_gather | solution.py:225
  1052.1 1173.9 %all-gather.22.cloned.1.call-start = ((), (), s32[]{:S(2)}) async-start(), calls=%async_computation.17 | async-start | bytes 2162688 | tf_op jit(solution)/shard_map/all_gather | solution.py:313
  1078.9 1150.9 %all-gather.20.cloned.1.call-start = ((), (), s32[]{:S(2)}) async-start(), calls=%async_computation.15 | async-start | bytes 4325376 | tf_op jit(solution)/shard_map/all_gather | solution.py:310
  1362.2 930.3 %reduce-scatter.5.cloned.1.call-start = ((), (), s32[]{:S(2)}) async-start(), calls=%async_computation.11 | async-start | bytes 9437184 | tf_op jit(solution)/shard_map/reduce_scatter | solution.py:290
  2202.9 126.1 %reduce-scatter.7.cloned.1.call-start = ((), (), s32[]{:S(2)}) async-start(), calls=%async_computation.13 | async-start | bytes 2359296 | tf_op jit(solution)/shard_map/reduce_scatter | solution.py:293
  2211.2 223.4 %all-reduce.125.cloned.1.call-start = ((), (), s32[]{:S(2)}) async-start(), calls=%async_computation.10 | async-start | bytes 8388608 | tf_op jit(solution)/shard_map/psum | solution.py:285
  2225.4 256.8 %all-gather.18.cloned.1.call-start = ((), (), s32[]{:S(2)}) async-start(), calls=%async_computation.12 | async-start | bytes 3145728 | tf_op jit(solution)/shard_map/all_gather | solution.py:304
  (201 other events, 1858.8 us)
Sparse Core Ops, SparseCore 0:
  10.5 152.3 all-gather.9
  164.4 44.1 all-gather.11
  494.9 170.3 all-reduce.120
  667.3 201.7 all-gather.13
  870.6 104.8 all-gather.15
  1002.3 63.0 reduce-scatter.10
  1069.4 170.4 all-reduce.122
  1242.2 119.9 reduce-scatter.8
  1364.6 155.7 all-gather.23
  1521.8 9.4 all-gather.21
  1532.9 12.9 all-gather.19
  2203.1 89.4 reduce-scatter.4
  2294.8 34.1 reduce-scatter.6
  2332.1 102.4 all-reduce.124
  2436.1 10.5 all-gather.17
